TPU v7x, 512 devices: a whole 4x8x8 slice. The times are simulated.
512 devices in a mesh: grp: 8 (over z_lo, x), tile: 64 (over y, z_hi, core).
Axes of the slice: x: 4, y: 8, z: 8 (z_hi: 4, z_lo: 2; z = z_hi * 2 + z_lo), core: 2. Of those that a mesh axis runs over, the one named last changes fastest.
Arguments:
- pixels: bfloat16 [512, 128, 3, 256], P(('grp', 'tile')), parts along dimension 0, may hold values from -6 to 6
- patch_weight: bfloat16 [768, 1024], P('tile'), may hold values from -0.21875 to 0.21875
- qkv_weight: bfloat16 [1024, 1536], P('tile'), may hold values from -2.0625 to 2.0625
- out_weight: bfloat16 [512, 1024], P('tile'), may hold values from -0.25 to 0.25
- reward_head: float32 [1024], replicated, may hold values from -4 to 4
- conv_weight: bfloat16 [3, 3, 48, 3], replicated, may hold values from -1.25 to 1.25
Outputs:
- rewards: float32 [512], P(('grp', 'tile')), parts along dimension 0
- act_grad: bfloat16 [512, 128, 48, 256], P('grp', 'tile'), parts along dimension 0
There are 8 independent parts, one for each index of `grp`. A program takes and returns all parts, laid end to end along the dimension named above; an argument that names none is the same for every part. Nothing has to cross between parts.
All inputs are finite; a program needn't handle non-finite values.
Results may differ from a plain program's by a relative error of at most 0.02.
Values may be sent and summed in bfloat16 or wider, within the bound.
No kernel may reach another device: no remote copies, remote signals or barrier semaphores. Data moves between devices by JAX's collectives and lax.ppermute only.
A program may use at most 64 MiB of HBM per device.

v0:
```python
import jax
import jax.numpy as jnp
from jax import lax
from jax.sharding import PartitionSpec as P

D = 1024
HEADS = 8
HEAD_DIM = 64
PATCH = 16
PDIM = 768
LOSS_SCALE = 1024.0
NORM_EPSILON = 1e-05


def extended(value, sides, width):
    for axis, dim in sides:
        devices, length = (lax.axis_size(axis), value.shape[dim])
        up = [(i, (i + 1) % devices) for i in range(devices - 1)]
        down = [(j, i) for i, j in up]
        last = lax.slice_in_dim(value, length - width, length, axis=dim)
        first = lax.slice_in_dim(value, 0, width, axis=dim)
        before = lax.ppermute(last, axis, up)
        after = lax.ppermute(first, axis, down)
        value = jnp.concatenate([before, value, after], axis=dim)
    return value


def normalize(values_in):
    average = jnp.mean(values_in, -1, keepdims=True)
    centred = values_in - average
    inverse_scale = lax.rsqrt(jnp.mean(centred * centred, -1, keepdims=True) + NORM_EPSILON)
    return (centred * inverse_scale, inverse_scale)


def norm_back(grad_in, normed, inverse_scale):
    return inverse_scale * (
        grad_in
        - jnp.mean(grad_in, -1, keepdims=True)
        - normed * jnp.mean(grad_in * normed, -1, keepdims=True)
    )


def to_patch_rows(pixels):
    frame_count, row_count, _, col_count = pixels.shape
    blocks = pixels.reshape(frame_count, row_count // PATCH, PATCH, 3, col_count // PATCH, PATCH)
    blocks = blocks.transpose(0, 1, 4, 3, 2, 5)
    return blocks.reshape(frame_count, row_count // PATCH * (col_count // PATCH), 3 * PATCH * PATCH)


def from_patch_rows(patches, row_count, col_count):
    frame_count = patches.shape[0]
    blocks = patches.reshape(frame_count, row_count // PATCH, col_count // PATCH, 3, PATCH, PATCH)
    blocks = blocks.transpose(0, 1, 4, 3, 2, 5)
    return blocks.reshape(frame_count, row_count, 3, col_count)


def attend_forward(spread, full_qkv):
    frame_count, local_count, model_width = spread.shape
    score_scale = HEAD_DIM ** (-0.5)
    first_normed, first_scale = normalize(spread.astype(jnp.float32))
    projected = jnp.dot(
        first_normed.astype(jnp.bfloat16).reshape(-1, model_width),
        full_qkv,
        preferred_element_type=jnp.float32,
    )
    projected = projected.astype(jnp.bfloat16).reshape(frame_count, local_count, 3, HEADS, HEAD_DIM)
    query_rows = projected[:, :, 0]
    key_rows = projected[:, :, 1]
    value_rows = projected[:, :, 2]
    scores = (
        jnp.einsum("iphd,jphd->phij", query_rows, key_rows, preferred_element_type=jnp.float32)
        * score_scale
    )
    attn_probs = jax.nn.softmax(scores, axis=-1)
    probs_rounded = attn_probs.astype(jnp.bfloat16)
    attended = jnp.einsum(
        "phij,jphd->iphd", probs_rounded, value_rows, preferred_element_type=jnp.float32
    )
    attended = attended.astype(jnp.bfloat16).reshape(frame_count, local_count, HEADS * HEAD_DIM)
    return (
        first_normed,
        first_scale,
        query_rows,
        key_rows,
        value_rows,
        attn_probs,
        probs_rounded,
        attended,
    )


def attend_backward(grad_spread, saved, back_qkv):
    first_normed, first_scale, query_rows, key_rows, value_rows, attn_probs, probs_rounded, _ = (
        saved
    )
    frame_count, local_count = (first_normed.shape[0], first_normed.shape[1])
    score_scale = HEAD_DIM ** (-0.5)
    grad_heads = grad_spread.reshape(frame_count, local_count, HEADS, HEAD_DIM)
    grad_probs = jnp.einsum(
        "iphd,jphd->phij", grad_heads, value_rows, preferred_element_type=jnp.float32
    )
    grad_value = jnp.einsum(
        "phij,iphd->jphd", probs_rounded, grad_heads, preferred_element_type=jnp.float32
    ).astype(jnp.bfloat16)
    row_delta = jnp.sum(attn_probs * grad_probs, -1, keepdims=True)
    grad_scores = (attn_probs * (grad_probs - row_delta) * score_scale).astype(jnp.bfloat16)
    grad_query = jnp.einsum(
        "phij,jphd->iphd", grad_scores, key_rows, preferred_element_type=jnp.float32
    ).astype(jnp.bfloat16)
    grad_key = jnp.einsum(
        "phij,iphd->jphd", grad_scores, query_rows, preferred_element_type=jnp.float32
    ).astype(jnp.bfloat16)
    grad_proj = jnp.stack([grad_query, grad_key, grad_value], 2).reshape(-1, 3 * HEADS * HEAD_DIM)
    grad_first = jnp.dot(grad_proj, back_qkv.T, preferred_element_type=jnp.float32)
    grad_first = grad_first.reshape(first_normed.shape)
    return norm_back(grad_first, first_normed, first_scale).astype(jnp.bfloat16)


def on_device(pixels, patch_weight, qkv_weight, out_weight, reward_head, conv_weight):
    local_frames, row_count, _, col_count = pixels.shape
    model_width = D
    inner_width = HEADS * HEAD_DIM
    full_patch, full_qkv, full_out = (
        lax.all_gather(patch_weight, "tile", axis=0, tiled=True),
        lax.all_gather(qkv_weight, "tile", axis=0, tiled=True),
        lax.all_gather(out_weight, "tile", axis=0, tiled=True),
    )
    patches = to_patch_rows(pixels)
    patch_count = patches.shape[1]
    spread_patches = lax.all_to_all(patches, "tile", split_axis=1, concat_axis=0, tiled=True)
    frame_count, local_count = (spread_patches.shape[0], spread_patches.shape[1])
    embedded = jnp.dot(
        spread_patches.reshape(-1, PDIM), full_patch, preferred_element_type=jnp.float32
    )
    embedded = embedded.astype(jnp.bfloat16).reshape(frame_count, local_count, model_width)
    saved = attend_forward(embedded, full_qkv)
    hidden = embedded.astype(jnp.float32) + jnp.dot(
        saved[7].reshape(-1, inner_width), full_out, preferred_element_type=jnp.float32
    ).reshape(embedded.shape)
    second_normed, second_scale = normalize(hidden)
    partial_sums = jnp.sum(jnp.sum(second_normed * reward_head, -1), -1)
    all_rewards = lax.psum(partial_sums, "tile") / patch_count
    rewards = lax.dynamic_slice_in_dim(
        all_rewards, lax.axis_index("tile") * local_frames, local_frames
    )
    frame_coeff = -LOSS_SCALE * jax.nn.sigmoid(-all_rewards)
    grad_second = frame_coeff[:, None, None] * reward_head / patch_count
    grad_hidden = norm_back(grad_second, second_normed, second_scale)
    hidden_rounded = grad_hidden.astype(jnp.bfloat16)
    back_patch, back_qkv, back_out = (
        lax.all_gather(patch_weight, "tile", axis=0, tiled=True),
        lax.all_gather(qkv_weight, "tile", axis=0, tiled=True),
        lax.all_gather(out_weight, "tile", axis=0, tiled=True),
    )
    grad_attended = jnp.dot(
        hidden_rounded.reshape(-1, model_width), back_out.T, preferred_element_type=jnp.float32
    )
    grad_attended = grad_attended.astype(jnp.bfloat16).reshape(
        hidden.shape[0], hidden.shape[1], inner_width
    )
    grad_embed = attend_backward(grad_attended, saved, back_qkv)
    grad_total = (grad_hidden + grad_embed.astype(jnp.float32)).astype(jnp.bfloat16)
    grad_patches = jnp.dot(
        grad_total.reshape(-1, model_width), back_patch.T, preferred_element_type=jnp.float32
    )
    grad_patches = grad_patches.astype(jnp.bfloat16).reshape(hidden.shape[0], hidden.shape[1], PDIM)
    home_patches = lax.all_to_all(grad_patches, "tile", split_axis=0, concat_axis=1, tiled=True)
    grad_pixels = from_patch_rows(home_patches, row_count, col_count)
    row_grad = lax.all_to_all(grad_pixels, "tile", split_axis=1, concat_axis=0, tiled=True)
    tile_rows = row_grad.shape[1]
    padded = extended(row_grad, (("tile", 1),), 1)
    padded = jnp.pad(padded, ((0, 0), (0, 0), (0, 0), (1, 1)))
    pieces = [
        padded[:, 2 - row_off : 2 - row_off + tile_rows, :, 2 - col_off : 2 - col_off + col_count]
        for row_off in range(3)
        for col_off in range(3)
    ]
    stacked = jnp.stack(pieces, 2).reshape(row_grad.shape[0], tile_rows, 27, col_count)
    kernel = conv_weight.transpose(0, 1, 3, 2).reshape(27, -1)
    act_grad = jnp.einsum(
        "fykx,kc->fycx", stacked, kernel, preferred_element_type=jnp.float32
    ).astype(jnp.bfloat16)
    return (rewards, act_grad)


def solution(mesh):
    in_specs = (
        P(("grp", "tile"), None, None, None),
        P("tile", None),
        P("tile", None),
        P("tile", None),
        P(),
        P(),
    )
    out_specs = (P(("grp", "tile")), P("grp", "tile", None, None))
    return jax.shard_map(
        on_device, mesh=mesh, in_specs=in_specs, out_specs=out_specs, check_vma=False
    )
```

profile of v0, /device:TPU:1, one launch (start us, length us, event | category | flops | bytes accessed | tf_op | source)
XLA Modules:
  0.0 508.4 jit_solution(12765785373744496446)
XLA Ops:
  8.6 2.1 reshape.213
  12.8 1.8 reduce.4
  15.3 17.6 %all-to-all-start = ((bf16[64,2,768]{2,1,0:T(2,128)(2,1)}), bf16[64,2,768]{2,1,0:T(2,128)(2,1)S(1)}, u32[]{:S(2)}, u32[]{:S(2)}) async-start(bf16[64,2,768]{2,1,0:T(2,128)(2,1)} %reshape.233), calls=%async_computation | async-start | bytes 393216 | tf_op jit(solution)/shard_map/all_to_all | solution.py:130
  33.7 14.1 %all-to-all-done = bf16[64,2,768]{2,1,0:T(2,128)(2,1)S(1)} async-done(((bf16[64,2,768]{2,1,0:T(2,128)(2,1)}), bf16[64,2,768]{2,1,0:T(2,128)(2,1)S(1)}, u32[]{:S(2)}, u32[]{:S(2)}) %all-to-all-start) | async-done | bytes 196640 | tf_op jit(solution)/shard_map/all_to_all | solution.py:130
  47.9 55.3 %all-gather.9.cloned.1.call-done = bf16[64,12,1024]{2,1,0:T(8,128)(2,1)} async-done(((bf16[1,12,1024]{2,1,0:T(8,128)(2,1)}), bf16[64,12,1024]{2,1,0:T(8,128)(2,1)}) %all-gather.9.cloned.1.call-update) | async-done | bytes 1572880 | tf_op jit(solution)/shard_map/all_gather | solution.py:124
  103.2 2.5 reshape.226
  107.7 81.3 %all-gather.5.cloned.1.call-done = bf16[1024,1536]{1,0:T(8,128)(2,1)} async-done(((bf16[16,1536]{1,0:T(8,128)(2,1)}), bf16[1024,1536]{1,0:T(8,128)(2,1)}) %all-gather.5.cloned.1.call-update) | async-done | bytes 3145744 | tf_op jit(solution)/shard_map/all_gather | solution.py:125
  189.0 2.5 convolution_convert_fusion
  195.4 76.6 %all-gather.7.cloned.1.call-done = bf16[512,1024]{1,0:T(8,128)(2,1)} async-done(((bf16[8,1024]{1,0:T(8,128)(2,1)}), bf16[512,1024]{1,0:T(8,128)(2,1)}) %all-gather.7.cloned.1.call-update) | async-done | bytes 1048592 | tf_op jit(solution)/shard_map/all_gather | solution.py:126
  272.0 1.7 fusion.55
  274.2 138.3 %psum.7 = f32[64]{0:T(128)S(1)} all-reduce(f32[64]{0:T(128)S(1)} %multiply_reduce_fusion.3), channel_id=1, replica_groups=mesh['grp'=8,'tile'=64] {'tile'}, use_global_device_ids=true, to_apply=%region_7.0 | all-reduce | flops 64 | bytes 512 | tf_op jit(solution)/shard_map/psum | solution.py:142
  414.6 1.7 convolution_convert_fusion.7
  417.9 2.7 fusion.13
  420.6 2.6 fusion.14
  426.0 1.8 dot_general.54
  427.8 3.2 fusion.50
  432.6 23.5 %all_to_all.30 = bf16[64,2,768]{2,1,0:T(2,128)(2,1)S(1)} all-to-all(bf16[64,2,768]{2,1,0:T(2,128)(2,1)S(1)} %reshape.219), channel_id=1, replica_groups=mesh['grp'=8,'tile'=64] {'tile'}, dimensions={0} | all-to-all | bytes 393216 | tf_op jit(solution)/shard_map/all_to_all | solution.py:167
  457.6 1.8 reshape.231
  459.4 19.2 %all_to_all.31 = bf16[1,128,3,256]{3,2,0,1:T(4,128)(2,1)S(1)} all-to-all(bf16[1,128,3,256]{3,2,0,1:T(4,128)(2,1)S(1)} %reshape.231), channel_id=1, replica_groups=mesh['grp'=8,'tile'=64] {'tile'}, dimensions={1} | all-to-all | bytes 393216 | tf_op jit(solution)/shard_map/all_to_all | solution.py:169
  479.1 3.3 collective-permute-start
  482.4 2.1 collective-permute-start.1
  485.2 8.7 %collective-permute-done.1 = bf16[64,1,3,256]{3,1,0,2:T(2,128)(2,1)S(1)} collective-permute-done((bf16[64,1,3,256]{3,1,0,2:T(2,128)(2,1)S(1)}, bf16[64,1,3,256]{3,1,0,2:T(2,128)(2,1)S(1)}, u32[]{:S(2)}, u32[]{:S(2)}) %collective-permute-start.1) | collective-permute-done | bytes 98336 | tf_op jit(solution)/shard_map/ppermute | solution.py:23
  493.8 1.8 select_maximum_fusion
  498.8 3.1 convert_bitcast_fusion
  (90 shorter events, 25.1 us)
Async XLA Ops:
  7.2 96.0 %all-gather.9.cloned.1.call-start = ((), (), s32[]{:S(2)}) async-start(), calls=%async_computation.5 | async-start | bytes 2129920 | tf_op jit(solution)/shard_map/all_gather | solution.py:124
  7.9 181.1 %all-gather.5.cloned.1.call-start = ((), (), s32[]{:S(2)}) async-start(), calls=%async_computation.3 | async-start | bytes 3194880 | tf_op jit(solution)/shard_map/all_gather | solution.py:125
  15.3 32.4 %all-to-all-start = ((bf16[64,2,768]{2,1,0:T(2,128)(2,1)}), bf16[64,2,768]{2,1,0:T(2,128)(2,1)S(1)}, u32[]{:S(2)}, u32[]{:S(2)}) async-start(bf16[64,2,768]{2,1,0:T(2,128)(2,1)} %reshape.233), calls=%async_computation | async-start | bytes 393216 | tf_op jit(solution)/shard_map/all_to_all | solution.py:130
  32.9 239.1 %all-gather.7.cloned.1.call-start = ((), (), s32[]{:S(2)}) async-start(), calls=%async_computation.4 | async-start | bytes 1064960 | tf_op jit(solution)/shard_map/all_gather | solution.py:126
  194.6 0.6 copy-start.10
  194.6 77.4 %copy-start.9 = (f32[2,8,64,64]{2,3,1,0:T(8,128)}, f32[2,8,64,64]{2,3,1,0:T(8,128)S(1)}, u32[]{:S(2)}) copy-start(f32[2,8,64,64]{2,3,1,0:T(8,128)S(1)} %get-tuple-element.16) | copy-start | bytes 786436
  195.4 78.5 %copy-start.5 = (f32[1024]{0:T(1024)S(1)}, f32[1024]{0:T(1024)}, u32[]{:S(2)}) copy-start(f32[1024]{0:T(1024)} %param.10) | copy-start | bytes 12292
  413.3 0.7 copy-start
  416.8 3.7 copy-start.2
  416.8 3.7 copy-start.11
  423.1 1.4 copy-start.3
  423.1 1.4 copy-start.4
  424.7 3.0 copy-start.7
  427.8 3.2 copy-start.1
  457.6 26.9 %copy-start.6 = (bf16[3,3,48,3]{2,3,1,0:T(4,128)(2,1)S(1)}, bf16[3,3,48,3]{2,3,1,0:T(4,128)(2,1)}, u32[]{:S(2)}) copy-start(bf16[3,3,48,3]{2,3,1,0:T(4,128)(2,1)} %param.11) | copy-start | bytes 7780
  457.6 26.9 %copy-start.8 = (f32[64]{0:T(128)S(1)}, f32[64]{0:T(128)}, u32[]{:S(2)}) copy-start(f32[64]{0:T(128)} %get-tuple-element.12) | copy-start | bytes 772
  479.1 6.1 %collective-permute-start = (bf16[64,1,3,256]{3,1,0,2:T(2,128)(2,1)S(1)}, bf16[64,1,3,256]{3,1,0,2:T(2,128)(2,1)S(1)}, u32[]{:S(2)}, u32[]{:S(2)}) collective-permute-start(bf16[64,1,3,256]{3,1,0,2:T(2,128)(2,1)S(1)} %get-tuple-element.7), channel_id=1, source_target_pairs={{0,1},{1,2},{2,3},{3,4},{4,5},{5,6},{6,7},{7,8},{8,9},{9,10},{10,1... | collective-permute-start | bytes 294920 | tf_op jit(solution)/shard_map/ppermute | solution.py:22
  482.4 11.5 %collective-permute-start.1 = (bf16[64,1,3,256]{3,1,0,2:T(2,128)(2,1)S(1)}, bf16[64,1,3,256]{3,1,0,2:T(2,128)(2,1)S(1)}, u32[]{:S(2)}, u32[]{:S(2)}) collective-permute-start(bf16[64,1,3,256]{3,1,0,2:T(2,128)(2,1)S(1)} %get-tuple-element.8), channel_id=1, source_target_pairs={{1,0},{2,1},{3,2},{4,3},{5,4},{6,5},{7,6},{8,7},{9,8},{10,9},{11,1... | collective-permute-start | bytes 294920 | tf_op jit(solution)/shard_map/ppermute | solution.py:23
Sparse Core Ops, SparseCore 0:
  11.3 91.8 all-gather.8
  106.5 82.4 all-gather.4
  192.3 79.6 all-gather.6
where the time goes:
time: 509 us; the launch traced here: 508 us
  waiting for transfers between devices  238 us (47%)
  blocking collectives  181 us (36%)
  starting transfers between devices  23.1 us (5%)
  matrix products  22.6 us (4%)
  local copies, waits for them, and re-layouts  22.4 us (4%)
  between operations  14.2 us (3%)
  other arithmetic  7.14 us (1%)
    psum x1, blocking collectives, on_device(): all_rewards = lax.psum(partial_sums, 'tile') / patch_count  138 us
    all_gather x1, waiting for transfers between devices, on_device(): lax.all_gather(qkv_weight, 'tile', axis=0, tiled=True)  81.3 us
    all_gather x1, waiting for transfers between devices, on_device(): lax.all_gather(out_weight, 'tile', axis=0, tiled=True)  76.6 us
    all_gather x1, waiting for transfers between devices, on_device(): lax.all_gather(patch_weight, 'tile', axis=0, tiled=True)  55.3 us
    all_to_all x1, blocking collectives, on_device(): lax.all_to_all(grad_patches, 'tile', split_axis=0, concat_axis=1, tiled=T...  23.5 us
    all_to_all x1, blocking collectives, on_device(): lax.all_to_all(grad_pixels, 'tile', split_axis=1, concat_axis=0, tiled=True)  19.2 us
    all_to_all x1, starting transfers between devices, on_device(): lax.all_to_all(patches, 'tile', split_axis=1, concat_axis=0, tiled=True)  17.6 us
    all_to_all x1, waiting for transfers between devices, on_device(): lax.all_to_all(patches, 'tile', split_axis=1, concat_axis=0, tiled=True)  14.1 us
  transfers between devices with their start and end apart: 6, of which 5 were waited for; matrix products, arithmetic and copies ran while one was open for 3% of the time, Pallas kernels for 0%

commit v1 on v0

--- a/solution.py
+++ b/solution.py
@@ -139,7 +139,7 @@
     ).reshape(embedded.shape)
     second_normed, second_scale = normalize(hidden)
     partial_sums = jnp.sum(jnp.sum(second_normed * reward_head, -1), -1)
-    all_rewards = lax.psum(partial_sums, "tile") / patch_count
+    all_rewards = jnp.sum(lax.all_gather(partial_sums, "tile"), axis=0) / patch_count
     rewards = lax.dynamic_slice_in_dim(
         all_rewards, lax.axis_index("tile") * local_frames, local_frames
     )

time: 509 us -> 646 us (1.27)
  blocking collectives: 181 us -> 317 us
    unnamed x0 -> x1, blocking collectives: none -> 272 us
    psum x1 -> x0, blocking collectives: 138 us -> none  [on_device(): all_rewards = lax.psum(partial_sums, 'tile') / patch_count]
where the time goes in v1:
time: 646 us; the launch traced here: 645 us
  blocking collectives  317 us (49%)
  waiting for transfers between devices  236 us (37%)
  local copies, waits for them, and re-layouts  24 us (4%)
  starting transfers between devices  23.1 us (4%)
  matrix products  22.6 us (3%)
  between operations  14.9 us (2%)
  other arithmetic  7.17 us (1%)
    unnamed x1, blocking collectives  272 us
    all_gather x1, waiting for transfers between devices, on_device(): lax.all_gather(qkv_weight, 'tile', axis=0, tiled=True)  81.3 us
    all_gather x1, waiting for transfers between devices, on_device(): lax.all_gather(out_weight, 'tile', axis=0, tiled=True)  76.6 us
    all_gather x1, waiting for transfers between devices, on_device(): lax.all_gather(patch_weight, 'tile', axis=0, tiled=True)  55.3 us
    all_to_all x1, blocking collectives, on_device(): lax.all_to_all(grad_patches, 'tile', split_axis=0, concat_axis=1, tiled=T...  26 us
    all_to_all x1, blocking collectives, on_device(): lax.all_to_all(grad_pixels, 'tile', split_axis=1, concat_axis=0, tiled=True)  19.2 us
    all_to_all x1, starting transfers between devices, on_device(): lax.all_to_all(patches, 'tile', split_axis=1, concat_axis=0, tiled=True)  17.6 us
  transfers between devices with their start and end apart: 6, of which 5 were waited for; matrix products, arithmetic and copies ran while one was open for 3% of the time, Pallas kernels for 0%

profile of v1, /device:TPU:1, one launch (start us, length us, event | category | flops | bytes accessed | tf_op | source)
XLA Modules:
  0.0 645.3 jit_solution(7740311417812628561)
XLA Ops:
  8.6 2.1 reshape.224
  12.8 1.8 reduce.4
  15.3 17.6 %all-to-all-start = ((bf16[64,2,768]{2,1,0:T(2,128)(2,1)}), bf16[64,2,768]{2,1,0:T(2,128)(2,1)S(1)}, u32[]{:S(2)}, u32[]{:S(2)}) async-start(bf16[64,2,768]{2,1,0:T(2,128)(2,1)} %reshape.250), calls=%async_computation | async-start | bytes 393216 | tf_op jit(solution)/shard_map/all_to_all | solution.py:130
  35.6 12.1 %all-to-all-done = bf16[64,2,768]{2,1,0:T(2,128)(2,1)S(1)} async-done(((bf16[64,2,768]{2,1,0:T(2,128)(2,1)}), bf16[64,2,768]{2,1,0:T(2,128)(2,1)S(1)}, u32[]{:S(2)}, u32[]{:S(2)}) %all-to-all-start) | async-done | bytes 196640 | tf_op jit(solution)/shard_map/all_to_all | solution.py:130
  47.9 55.3 %all-gather.10.cloned.1.call-done = bf16[64,12,1024]{2,1,0:T(8,128)(2,1)} async-done(((bf16[1,12,1024]{2,1,0:T(8,128)(2,1)}), bf16[64,12,1024]{2,1,0:T(8,128)(2,1)}) %all-gather.10.cloned.1.call-update) | async-done | bytes 1572880 | tf_op jit(solution)/shard_map/all_gather | solution.py:124
  103.2 2.5 reshape.241
  107.7 81.3 %all-gather.6.cloned.1.call-done = bf16[1024,1536]{1,0:T(8,128)(2,1)} async-done(((bf16[16,1536]{1,0:T(8,128)(2,1)}), bf16[1024,1536]{1,0:T(8,128)(2,1)}) %all-gather.6.cloned.1.call-update) | async-done | bytes 3145744 | tf_op jit(solution)/shard_map/all_gather | solution.py:125
  189.0 2.5 convolution_convert_fusion
  195.4 76.6 %all-gather.8.cloned.1.call-done = bf16[512,1024]{1,0:T(8,128)(2,1)} async-done(((bf16[8,1024]{1,0:T(8,128)(2,1)}), bf16[512,1024]{1,0:T(8,128)(2,1)}) %all-gather.8.cloned.1.call-update) | async-done | bytes 1048592 | tf_op jit(solution)/shard_map/all_gather | solution.py:126
  272.0 1.7 fusion.55
  274.5 272.2 %all-reduce.1 = f32[4096]{0:T(1024)S(1)} all-reduce(f32[4096]{0:T(1024)S(1)} %dynamic-update-slice), channel_id=2, replica_groups=mesh['grp'=8,'tile'=64] {'tile'}, use_global_device_ids=true, to_apply=%add.1 | all-reduce | flops 4096 | bytes 32768
  548.9 1.7 convolution_convert_fusion.7
  552.2 2.7 fusion.13
  554.9 2.6 fusion.14
  560.4 1.8 dot_general.54
  562.1 3.2 fusion.50
  566.9 26.0 %all_to_all.30 = bf16[64,2,768]{2,1,0:T(2,128)(2,1)S(1)} all-to-all(bf16[64,2,768]{2,1,0:T(2,128)(2,1)S(1)} %reshape.230), channel_id=1, replica_groups=mesh['grp'=8,'tile'=64] {'tile'}, dimensions={0} | all-to-all | bytes 393216 | tf_op jit(solution)/shard_map/all_to_all | solution.py:167
  594.5 1.8 reshape.248
  596.3 19.2 %all_to_all.31 = bf16[1,128,3,256]{3,2,0,1:T(4,128)(2,1)S(1)} all-to-all(bf16[1,128,3,256]{3,2,0,1:T(4,128)(2,1)S(1)} %reshape.248), channel_id=1, replica_groups=mesh['grp'=8,'tile'=64] {'tile'}, dimensions={1} | all-to-all | bytes 393216 | tf_op jit(solution)/shard_map/all_to_all | solution.py:169
  616.0 3.3 collective-permute-start
  619.3 2.1 collective-permute-start.1
  622.0 8.7 %collective-permute-done.1 = bf16[64,1,3,256]{3,1,0,2:T(2,128)(2,1)S(1)} collective-permute-done((bf16[64,1,3,256]{3,1,0,2:T(2,128)(2,1)S(1)}, bf16[64,1,3,256]{3,1,0,2:T(2,128)(2,1)S(1)}, u32[]{:S(2)}, u32[]{:S(2)}) %collective-permute-start.1) | collective-permute-done | bytes 98336 | tf_op jit(solution)/shard_map/ppermute | solution.py:23
  630.7 1.8 select_maximum_fusion
  635.7 3.1 convert_bitcast_fusion
  (95 shorter events, 26.7 us)
Async XLA Ops:
  7.2 96.0 %all-gather.10.cloned.1.call-start = ((), (), s32[]{:S(2)}) async-start(), calls=%async_computation.5 | async-start | bytes 2129920 | tf_op jit(solution)/shard_map/all_gather | solution.py:124
  7.9 181.1 %all-gather.6.cloned.1.call-start = ((), (), s32[]{:S(2)}) async-start(), calls=%async_computation.3 | async-start | bytes 3194880 | tf_op jit(solution)/shard_map/all_gather | solution.py:125
  15.3 32.4 %all-to-all-start = ((bf16[64,2,768]{2,1,0:T(2,128)(2,1)}), bf16[64,2,768]{2,1,0:T(2,128)(2,1)S(1)}, u32[]{:S(2)}, u32[]{:S(2)}) async-start(bf16[64,2,768]{2,1,0:T(2,128)(2,1)} %reshape.250), calls=%async_computation | async-start | bytes 393216 | tf_op jit(solution)/shard_map/all_to_all | solution.py:130
  32.9 239.1 %all-gather.8.cloned.1.call-start = ((), (), s32[]{:S(2)}) async-start(), calls=%async_computation.4 | async-start | bytes 1064960 | tf_op jit(solution)/shard_map/all_gather | solution.py:126
  194.6 0.6 copy-start.10
  194.6 77.4 %copy-start.9 = (f32[2,8,64,64]{2,3,1,0:T(8,128)}, f32[2,8,64,64]{2,3,1,0:T(8,128)S(1)}, u32[]{:S(2)}) copy-start(f32[2,8,64,64]{2,3,1,0:T(8,128)S(1)} %get-tuple-element.16) | copy-start | bytes 786436
  195.4 78.5 %copy-start.5 = (f32[1024]{0:T(1024)S(1)}, f32[1024]{0:T(1024)}, u32[]{:S(2)}) copy-start(f32[1024]{0:T(1024)} %param.10) | copy-start | bytes 12292
  547.6 0.7 copy-start
  551.1 3.7 copy-start.2
  551.2 3.7 copy-start.11
  557.5 1.4 copy-start.3
  557.5 1.4 copy-start.4
  559.1 3.0 copy-start.7
  562.1 3.2 copy-start.1
  594.5 26.9 %copy-start.6 = (bf16[3,3,48,3]{2,3,1,0:T(4,128)(2,1)S(1)}, bf16[3,3,48,3]{2,3,1,0:T(4,128)(2,1)}, u32[]{:S(2)}) copy-start(bf16[3,3,48,3]{2,3,1,0:T(4,128)(2,1)} %param.11) | copy-start | bytes 7780
  594.5 26.9 %copy-start.8 = (f32[64]{0:T(128)S(1)}, f32[64]{0:T(128)}, u32[]{:S(2)}) copy-start(f32[64]{0:T(128)} %get-tuple-element.12) | copy-start | bytes 772
  616.0 6.1 collective-permute-start
  619.3 11.5 %collective-permute-start.1 = (bf16[64,1,3,256]{3,1,0,2:T(2,128)(2,1)S(1)}, bf16[64,1,3,256]{3,1,0,2:T(2,128)(2,1)S(1)}, u32[]{:S(2)}, u32[]{:S(2)}) collective-permute-start(bf16[64,1,3,256]{3,1,0,2:T(2,128)(2,1)S(1)} %get-tuple-element.8), channel_id=1, source_target_pairs={{1,0},{2,1},{3,2},{4,3},{5,4},{6,5},{7,6},{8,7},{9,8},{10,9},{11,1... | collective-permute-start | bytes 294920 | tf_op jit(solution)/shard_map/ppermute | solution.py:23
Sparse Core Ops, SparseCore 0:
  11.3 91.8 all-gather.9
  106.5 82.4 all-gather.5
  192.3 79.6 all-gather.7
